TPU v7x, 32 devices: a whole 2x2x4 slice. The times are simulated.
32 devices in a mesh: sims: 4 (over x, core), blk: 8 (over z, y).
Axes of the slice: x: 2, y: 2, z: 4, core: 2. Of those that a mesh axis runs over, the one named last changes fastest.
Arguments:
- sim_alm: bfloat16 [1536, 16, 2, 1536], P('blk', 'sims'), may hold values from -6 to 6
- t_filter: float32 [1536], replicated, may hold values from 0.0006510417 to 0.00390625
- wiener_filter: float32 [1536], replicated, may hold values from 8.477105e-07 to 5.086263e-06
- colatitude: float32 [16], replicated, may hold values from 1.18672 to 1.51328, as said below
- legendre: bfloat16 [1536, 1536, 16], P('blk'), may hold values from -2 to 2, as said below
- pixel_mask: int32 [16, 4096], P('blk'), may hold values 0 or 1
Outputs:
- field_sum: float32 [1536, 2, 1536], P('blk', None, 'sims')
- spectra: float32 [16, 2, 1536], P('sims')
Inputs may be any that keep to these rules, and one draw needn't show every extreme that they name: `colatitude`: the colatitudes of 16 cycles in increasing order, about 0.0016 apart, in a band centred between 1.2 and 1.5. legendre[m,l,r] is the orthonormal associated Legendre function of degree l and order m at colatitude[r], zero for l < m, rounded to bfloat16.
All inputs are finite; a program needn't handle non-finite values. No bound on the sum of `pixel_mask` on one device may be relied on, other than what follows from the above.
Results may differ from a plain program's by a relative error of at most 0.006.
The roundings to bfloat16 on the way count: a program that leaves them out, or rounds other values in their place, can miss the bound.
Values may be sent and summed in bfloat16 or wider, within the bound.
A program may use at most 192 MiB of HBM per device.

v0:
```python
import math

import jax
import jax.numpy as jnp
from jax import lax
from jax.sharding import PartitionSpec as P


def ladder(degree, orders):
    numerator = (2.0 * degree + 1.0) * (degree * degree - orders * orders)
    denominator = jnp.maximum(2.0 * degree - 1.0, 1.0)
    return jnp.where(degree > orders, jnp.sqrt(jnp.maximum(numerator, 0.0) / denominator), 0.0)


def fourier_table(mode_count, pixels):
    mode_ids = jnp.arange(mode_count, dtype=jnp.int32)[:, None]
    pixel_ids = jnp.arange(pixels, dtype=jnp.int32)[None, :]
    phases = 2.0 * math.pi / pixels * (mode_ids * pixel_ids % pixels).astype(jnp.float32)
    return jnp.stack(
        [jnp.cos(phases).astype(jnp.bfloat16), (-jnp.sin(phases)).astype(jnp.bfloat16)], axis=1
    )


def per_device(sim_alm, t_filter, wiener_filter, colatitude, legendre, pixel_mask):
    local_modes = sim_alm.shape[0]
    sims_here = sim_alm.shape[1]
    degrees = sim_alm.shape[3]
    cycle_count = legendre.shape[2]
    pixels = pixel_mask.shape[1]
    blocks = lax.axis_size("blk")
    cycle_local = cycle_count // blocks
    first_mode = lax.axis_index("blk") * local_modes
    degree = jnp.arange(degrees, dtype=jnp.float32)
    local_orders = (first_mode + jnp.arange(local_modes, dtype=jnp.int32)).astype(jnp.float32)
    all_orders = jnp.arange(degrees, dtype=jnp.float32)
    ladder_steps = ladder(degree[None, :], local_orders[:, None])
    cotangent = jnp.cos(colatitude) / jnp.sin(colatitude)
    cosecant = 1.0 / jnp.sin(colatitude)
    tilt_grid = jnp.cos(colatitude).reshape(blocks, 1, cycle_local)
    values = sim_alm.astype(jnp.float32)
    weighted = wiener_filter * values
    raised = ladder_steps[:, None, None, :] * weighted
    lowered = jnp.concatenate([raised[..., 1:], jnp.zeros_like(raised[..., :1])], axis=-1)
    coefs = jnp.stack([t_filter * values, weighted, degree * weighted, lowered], axis=1).astype(
        jnp.bfloat16
    )
    flattened = coefs.reshape(local_modes, 8 * sims_here, degrees)
    legsum = jnp.einsum("mkl,mlr->krm", flattened, legendre, preferred_element_type=jnp.float32)
    legsum = legsum.reshape(4, sims_here, 2, cycle_count, local_modes)
    rotated = jnp.stack([-legsum[1][:, 1], legsum[1][:, 0]], axis=1) * (
        cosecant[:, None] * local_orders[None, :]
    )
    slopes = cotangent[:, None] * legsum[2] - cosecant[:, None] * legsum[3]
    cycle_coefs = jnp.stack([legsum[0], rotated, slopes], axis=0).astype(jnp.bfloat16)
    cycle_coefs = cycle_coefs.reshape(3, sims_here, 2, cycle_count * local_modes)
    fourier = fourier_table(degrees, pixels)
    fourier_grid = fourier.reshape(blocks, local_modes, 2, pixels)
    mode_weight = (
        jnp.where(all_orders > 0, 2.0, 1.0).astype(jnp.bfloat16).reshape(blocks, 1, local_modes)
    )
    pixel_weight = pixel_mask.astype(jnp.float32)
    legendre_grid = legendre.reshape(local_modes, degrees, blocks, cycle_local)
    arranged = lax.all_to_all(cycle_coefs, "blk", split_axis=3, concat_axis=3, tiled=True).reshape(
        3, -1, 2, blocks, cycle_local, local_modes
    )
    scaled = arranged * mode_weight
    cycle_maps = jnp.einsum(
        "qscbrn,bncj->qsrj", scaled, fourier_grid, preferred_element_type=jnp.float32
    )
    product = pixel_weight * cycle_maps[0]
    flow_maps = jnp.stack([product * cycle_maps[2], product * cycle_maps[1]]).astype(jnp.bfloat16)
    mode_coefs = jnp.einsum(
        "psrj,mcj->pscmr", flow_maps, fourier, preferred_element_type=jnp.float32
    )
    mode_coefs = (mode_coefs * (2.0 * math.pi / pixels)).astype(jnp.bfloat16)
    mode_coefs = mode_coefs.reshape(2, mode_coefs.shape[1], 2, degrees * cycle_local)
    returned = lax.all_to_all(mode_coefs, "blk", split_axis=3, concat_axis=3, tiled=True)
    returned = returned.reshape(2, -1, 2, blocks, local_modes, cycle_local)
    tilted = (tilt_grid * returned[0].astype(jnp.float32)).astype(jnp.bfloat16)
    stacked = jnp.stack([tilted, returned[0], returned[1]], axis=0)
    projected = jnp.einsum(
        "kscbnr,nlbr->knscl", stacked, legendre_grid, preferred_element_type=jnp.float32
    )
    shifted = jnp.concatenate(
        [jnp.zeros_like(projected[1][..., :1]), projected[1][..., :-1]], axis=-1
    )
    first_part = projected[0]
    third_part = projected[2]
    order_column = local_orders[:, None, None]
    step_rows = ladder_steps[:, None, :]
    real_part = (
        degree * first_part[:, :, 0]
        - step_rows * shifted[:, :, 0]
        + order_column * third_part[:, :, 1]
    )
    imag_part = (
        degree * first_part[:, :, 1]
        - step_rows * shifted[:, :, 1]
        - order_column * third_part[:, :, 0]
    )
    estimates = jnp.stack([real_part, imag_part], axis=2) / degrees
    partial_value = jnp.sum(estimates, axis=1)
    quarter = degrees // lax.axis_size("sims")
    field_total = lax.psum(partial_value, "sims")
    field_share = lax.dynamic_slice_in_dim(
        field_total, lax.axis_index("sims") * quarter, quarter, 2
    )
    sim_total = sims_here * lax.axis_size("sims")
    residual = estimates - field_total[:, None] / sim_total
    partner = residual.reshape(local_modes, sims_here // 2, 2, 2, degrees)[:, :, ::-1].reshape(
        residual.shape
    )
    auto_power = jnp.sum(residual * residual, axis=2)
    cross_power = jnp.sum(residual * partner, axis=2)
    local_weight = jnp.where(local_orders > 0, 2.0, 1.0)
    local_power = jnp.stack(
        [
            jnp.einsum("m,msl->sl", local_weight, auto_power),
            jnp.einsum("m,msl->sl", local_weight, cross_power),
        ],
        axis=1,
    )
    summed = lax.psum(local_power, "blk")
    spectra = summed / (2.0 * degree + 1.0)
    return (field_share, spectra)


def solution(mesh):
    placed = (P("blk", "sims", None, None), P(), P(), P(), P("blk", None, None), P("blk", None))
    return jax.shard_map(
        per_device,
        mesh=mesh,
        in_specs=placed,
        out_specs=(P("blk", None, "sims"), P("sims", None, None)),
        check_vma=False,
    )
```

profile of v0, /device:TPU:0, one launch (start us, length us, event | category | flops | bytes accessed | tf_op | source)
XLA Modules:
  0.0 771.7 jit_solution(14534885427745455265)
XLA Ops:
  9.8 19.5 %convert_bitcast_fusion = (bf16[192,1,4,2,1536]{4,3,2,0,1:T(2,128)(2,1)}, bf16[192,1,4,2,1536]{4,3,2,0,1:T(2,128)(2,1)}, f32[192,4,2,1536]{3,2,1,0:T(2,128)S(1)}, bf16[192,1,4,2,1536]{4,3,2,0,1:T(2,128)(2,1)}) fusion(bf16[192,4,2,1536]{3,2,1,0:T(2,128)(2,1)} %param.6, f32[1536]{0:T(1024)} %param.8, f32[1536]{0:T(1024)} %param.7), kind=kLoop, calls=%fused_computation.61 | loop fusion | flops 16515072 | bytes 28323840 | tf_op jit(solution)/shard_map/stack | solution.py:44
  29.3 11.6 %fusion.15 = bf16[192,4,2,1535]{3,2,1,0:T(2,128)(2,1)} fusion(f32[192,4,2,1536]{3,2,1,0:T(2,128)S(1)} %get-tuple-element.19, f32[192,1535]{1,0:T(8,128)S(1)} %slice.101), kind=kLoop, calls=%fused_computation.35 | loop fusion | flops 4715520 | bytes 15325440 | tf_op jit(solution)/shard_map/convert.14
  40.9 8.8 %pad_bitcast_fusion = bf16[192,1,4,2,1536]{4,3,2,0,1:T(2,128)(2,1)} fusion(bf16[192,4,2,1535]{3,2,1,0:T(2,128)(2,1)} %fusion.15), kind=kLoop, calls=%fused_computation.60 | loop fusion | bytes 9434112 | tf_op jit(solution)/shard_map/stack | solution.py:44
  49.7 36.7 %pad_maximum_fusion = bf16[192,4,4,2,1536]{4,3,2,0,1:T(2,128)(2,1)S(1)} fusion(bf16[192,1,4,2,1536]{4,3,2,0,1:T(2,128)(2,1)} %pad_bitcast_fusion, bf16[192,1,4,2,1536]{4,3,2,0,1:T(2,128)(2,1)} %get-tuple-element.18, bf16[192,1,4,2,1536]{4,3,2,0,1:T(2,128)(2,1)} %get-tuple-element.17, bf16[192,1,4,2,1536]{4,3,2,0,1:T(2,128)(2,1)} %get-tuple-element.20), kind=kLoop, calls=%fused_computation.26 | loop fusion | flops 28311552 | bytes 37748736 | tf_op jit(solution)/shard_map/stack | solution.py:44
  86.4 19.4 %copy.102 = bf16[192,4,4,2,1536]{4,3,2,1,0:T(2,128)(2,1)} copy(bf16[192,4,4,2,1536]{4,3,2,0,1:T(2,128)(2,1)S(1)} %pad_maximum_fusion) | data formatting | bytes 37748736 | tf_op jit(solution)/shard_map/stack | solution.py:44
  105.8 38.3 %convert_element_type.140 = bf16[192,32,1536]{2,1,0:T(8,128)(2,1)} reshape(bf16[192,4,4,2,1536]{4,3,2,1,0:T(2,128)(2,1)} %copy.102) | data formatting | bytes 37748736 | tf_op jit(solution)/shard_map/convert_element_type | solution.py:44
  144.0 11.8 %convolution_bitcast_fusion.1 = f32[32,16,192]{0,1,2:T(8,128)S(1)} fusion(bf16[192,32,1536]{2,1,0:T(8,128)(2,1)} %convert_element_type.140, bf16[192,1536,16]{1,2,0:T(8,128)(2,1)} %param.10), kind=kOutput, calls=%fused_computation.67 | convolution fusion | flops 301989888 | bytes 28704768 | tf_op jit(solution)/shard_map/mkl,mlr->krm/dot_general | solution.py:48
  166.4 8.1 %copy.109 = bf16[3,4,2,3072]{1,2,0,3:T(2,128)(2,1)} copy(bf16[3,4,2,3072]{3,2,1,0:T(2,128)(2,1)S(1)} %pad_maximum_fusion.2) | data formatting | bytes 294912 | tf_op jit(solution)/shard_map/stack | solution.py:54
  174.5 10.3 %reshape.506 = bf16[8,2,4608]{2,1,0:T(2,128)(2,1)} reshape(bf16[3072,3,2,4]{3,2,1,0:T(2,128)(2,1)} %bitcast.98) | data formatting | bytes 294912
  184.8 7.7 %all-to-all-start = ((bf16[8,2,4608]{2,1,0:T(2,128)(2,1)}), bf16[8,2,4608]{2,1,0:T(2,128)(2,1)S(1)}, u32[]{:S(2)}, u32[]{:S(2)}) async-start(bf16[8,2,4608]{2,1,0:T(2,128)(2,1)} %reshape.506), calls=%async_computation | async-start | bytes 294912 | tf_op jit(solution)/shard_map/all_to_all | solution.py:63
  192.5 101.2 %negate_convert_fusion.1 = (bf16[1536,1,4096]{2,0,1:T(8,128)(2,1)}, bf16[1536,1,4096]{2,0,1:T(8,128)(2,1)}) fusion(), kind=kLoop, calls=%fused_computation.18 | loop fusion | flops 106954752 | bytes 25165824 | tf_op jit(solution)/shard_map/convert_element_type | solution.py:20
  293.7 104.7 %cosine_convert_fusion = (bf16[8,192,1,4096]{3,1,2,0:T(8,128)(2,1)}, bf16[8,192,1,4096]{3,1,2,0:T(8,128)(2,1)}) fusion(s32[8,192]{1,0:T(8,128)S(1)} %multiply_add_fusion), kind=kLoop, calls=%fused_computation.15 | loop fusion | flops 106954752 | bytes 25171968 | tf_op jit(solution)/shard_map/convert_element_type | solution.py:20
  398.5 11.0 %reshape.507 = bf16[3072,3,2,4]{3,2,1,0:T(2,128)(2,1)} reshape(bf16[8,2,4608]{2,1,0:T(2,128)(2,1)S(1)} %all-to-all-done) | data formatting | bytes 294912
  409.4 14.2 %copy.134 = bf16[3,4,2,8,2,192]{5,4,3,2,1,0:T(2,128)(2,1)S(1)} copy(bf16[3,4,2,8,2,192]{1,2,0,5,4,3:T(2,128)(2,1)} %bitcast.99) | data formatting | bytes 294912 | tf_op jit(solution)/shard_map/reshape | solution.py:63
  423.8 10.3 %fusion.29 = f32[3,4,2,4096]{3,1,2,0:T(4,128)S(1)} fusion(bf16[8,192,1,4096]{3,1,2,0:T(8,128)(2,1)} %get-tuple-element.31, bf16[8,192,1,4096]{3,1,2,0:T(8,128)(2,1)} %get-tuple-element.30, bf16[3,4,2,8,2,192]{5,4,3,2,1,0:T(2,128)(2,1)S(1)} %broadcast_multiply_fusion.1), kind=kOutput, calls=%fused_computation.62 | convolution fusion | flops 616562688 | bytes 25706496 | tf_op jit(solution)/shard_map/qscbrn,bncj->qsrj/dot_general | solution.py:67
  434.2 11.8 %fusion.32 = bf16[2,4,2,1536,2]{3,1,4,0,2:T(4,128)(2,1)S(1)} fusion(bf16[1536,1,4096]{2,0,1:T(8,128)(2,1)} %get-tuple-element.38, bf16[1536,1,4096]{2,0,1:T(8,128)(2,1)} %get-tuple-element.39, bf16[1,4,2,4096]{3,1,2,0:T(4,128)(2,1)S(1)} %get-tuple-element.27, bf16[1,4,2,4096]{3,1,2,0:T(4,128)(2,1)S(1)} %get-tuple-element.26), kind=kOutput, calls=%fused_computation.65 | convolution fusion | flops 453345280 | bytes 25395200 | tf_op jit(solution)/shard_map/psrj,mcj->pscmr/dot_general | solution.py:72
  448.7 20.8 %copy.153 = bf16[2,4,2,3072]{1,2,0,3:T(2,128)(2,1)} copy(bf16[2,4,2,3072]{1,3,2,0:T(8,128)(2,1)S(1)} %bitcast.101) | data formatting | bytes 196608 | tf_op jit(solution)/shard_map/reshape | solution.py:76
  469.5 9.2 %reshape.508 = bf16[8,2,3072]{2,1,0:T(2,128)(2,1)} reshape(bf16[3072,2,2,4]{3,2,1,0:T(2,128)(2,1)} %bitcast.102) | data formatting | bytes 196608
  484.8 19.2 %reshape.495 = bf16[192,1536,8,2]{1,3,2,0:T(2,128)(2,1)} reshape(bf16[192,1536,16]{1,2,0:T(8,128)(2,1)} %param.10) | data formatting | bytes 18874368 | tf_op jit(solution)/shard_map/reshape | solution.py:62
  504.1 6.7 reshape.509
  520.8 17.5 %convolution_bitcast_fusion = f32[3,192,4,2,1536]{4,2,3,0,1:T(4,128)} fusion(bf16[3,4,2,8,192,2]{3,1,5,2,0,4:T(4,128)(2,1)S(1)} %copy.119, bf16[192,1536,8,2,1,1]{1,3,2,0,5,4:T(2,128)(2,1)} %bitcast.92), kind=kOutput, calls=%fused_computation.27 | convolution fusion | flops 226492416 | bytes 37896192 | tf_op jit(solution)/shard_map/kscbnr,nlbr->knscl/dot_general | solution.py:81
  538.3 18.8 %slice_bitcast_fusion.2 = (f32[192,4,2,1536]{3,1,2,0:T(4,128)S(1)}, f32[192,4,2,1536]{3,1,2,0:T(4,128)}, f32[192,4,2,1536]{3,1,2,0:T(4,128)}) fusion(f32[3,192,4,2,1536]{4,2,3,0,1:T(4,128)} %convolution_bitcast_fusion), kind=kLoop, calls=%fused_computation.33 | loop fusion | bytes 56623104 | tf_op jit(solution)/shard_map/squeeze | solution.py:87
  557.1 9.3 %fusion.21 = (f32[192,4,1,1536]{3,1,2,0:T(4,128)S(1)}, f32[192,4,1,1536]{3,1,2,0:T(4,128)S(1)}) fusion(f32[192,4,2,1535]{3,1,2,0:T(4,128)} %bitcast.97, f32[192,4,2,1536]{3,1,2,0:T(4,128)} %get-tuple-element.15, f32[192,4,2,1536]{3,1,2,0:T(4,128)S(1)} %get-tuple-element.14, f32[192]{0:T(256)S(1)} %add_convert_fusion, f32[192,1536]{1,0:T(8,128)S(1)} %copy-done.3), kind=kLoop, calls=%fused_computation.48 | loop fusion | flops 11796480 | bytes 38923008 | tf_op jit(solution)/shard_map/add | solution.py:92
  570.0 10.2 %fusion.18 = f32[192,2,1536]{2,1,0:T(2,128)} fusion(f32[192,4,1,1536]{3,1,2,0:T(4,128)S(1)} %get-tuple-element.13, f32[192,4,1,1536]{3,1,2,0:T(4,128)S(1)} %get-tuple-element.12), kind=kLoop, calls=%fused_computation.45 | loop fusion | flops 6488064 | bytes 11796480 | tf_op jit(solution)/shard_map/reduce_sum | solution.py:102
  580.3 7.1 stack.88
  587.4 7.2 stack.89
  594.5 42.9 %all-reduce.4.cloned.1.call-done = f32[192,2,1536]{2,1,0:T(2,128)} async-done(((f32[192,2,1536]{2,1,0:T(2,128)}), f32[192,2,1536]{2,1,0:T(2,128)}) %all-reduce.4.cloned.1.call-update) | async-done | bytes 2359312 | tf_op jit(solution)/shard_map/psum | solution.py:104
  640.3 8.8 %multiply_reduce_fusion.1 = bf16[192,4,1536]{2,1,0:T(4,128)(2,1)S(1)} fusion(f32[192,4,1,1536]{3,1,2,0:T(4,128)} %copy-done.1, f32[192,4,1,1536]{3,1,2,0:T(4,128)} %copy-done, f32[192,2,1536]{2,1,0:T(2,128)S(1)} %broadcast_multiply_fusion), kind=kLoop, calls=%fused_computation.41 | loop fusion | flops 10616832 | bytes 14155776 | tf_op jit(solution)/shard_map/reduce_sum | solution.py:113
  650.4 9.8 %fusion.16 = f32[192,2,2,2,1536]{4,2,1,0,3:T(2,128)} fusion(f32[192,2,2,1,1536]{4,2,1,0,3:T(2,128)S(1)} %bitcast.96, f32[192,2,2,1,1536]{4,2,1,0,3:T(2,128)S(1)} %bitcast.94, f32[192,2,1536]{2,0,1:T(8,128)S(1)} %copy.123), kind=kLoop, calls=%fused_computation.38 | loop fusion | flops 7077888 | bytes 21233664 | tf_op jit(solution)/shard_map/sub | solution.py:109
  660.2 45.9 %rev.3 = f32[192,2,2,2,1536]{4,2,1,0,3:T(2,128)} reverse(f32[192,2,2,2,1536]{4,2,1,0,3:T(2,128)} %fusion.16), dimensions={2} | reverse | bytes 18874368 | tf_op jit(solution)/shard_map/rev | solution.py:110
  706.1 17.0 %multiply_reduce_fusion = bf16[192,2,2,1536]{3,2,1,0:T(2,128)(2,1)S(1)} fusion(f32[192,2,2,2,1536]{4,2,1,0,3:T(2,128)} %rev.3, f32[192,2,1536]{2,0,1:T(8,128)S(1)} %copy.123, f32[192,2,2,1,1536]{4,2,1,0,3:T(2,128)} %stack.89, f32[192,2,2,1,1536]{4,2,1,0,3:T(2,128)} %stack.88), kind=kLoop, calls=%fused_computation.40 | loop fusion | flops 10616832 | bytes 23592960 | tf_op jit(solution)/shard_map/reduce_sum | solution.py:114
  724.0 37.6 %psum.15 = f32[4,2,1536]{2,0,1:T(4,128)S(1)} all-reduce(f32[4,2,1536]{2,0,1:T(4,128)S(1)} %pad_maximum_fusion.3), channel_id=1, replica_groups=mesh['sims'=4,'blk'=8] {'blk'}, use_global_device_ids=true, to_apply=%region_4.5 | all-reduce | flops 12288 | bytes 98304 | tf_op jit(solution)/shard_map/psum | solution.py:123
  (88 shorter events, 43.4 us)
Async XLA Ops:
  7.2 0.6 copy-start.4
  8.4 1.0 copy-start.2
  155.9 5.8 copy-start.7
  184.8 213.7 %all-to-all-start = ((bf16[8,2,4608]{2,1,0:T(2,128)(2,1)}), bf16[8,2,4608]{2,1,0:T(2,128)(2,1)S(1)}, u32[]{:S(2)}, u32[]{:S(2)}) async-start(bf16[8,2,4608]{2,1,0:T(2,128)(2,1)} %reshape.506), calls=%async_computation | async-start | bytes 294912 | tf_op jit(solution)/shard_map/all_to_all | solution.py:63
  293.7 104.7 %copy-start.6 = (s32[2,4096]{1,0:T(2,128)S(1)}, s32[2,4096]{1,0:T(2,128)}, u32[]{:S(2)}) copy-start(s32[2,4096]{1,0:T(2,128)} %param.11) | copy-start | bytes 98308
  478.7 25.4 %all-to-all-start.1 = ((bf16[8,2,3072]{2,1,0:T(2,128)(2,1)}), bf16[8,2,3072]{2,1,0:T(2,128)(2,1)S(1)}, u32[]{:S(2)}, u32[]{:S(2)}) async-start(bf16[8,2,3072]{2,1,0:T(2,128)(2,1)} %reshape.508), calls=%async_computation.1 | async-start | bytes 196608 | tf_op jit(solution)/shard_map/all_to_all | solution.py:77
  484.7 152.7 %all-reduce.4.cloned.1.call-start = ((), (), s32[]{:S(2)}) async-start(), calls=%async_computation.2 | async-start | bytes 4718592 | tf_op jit(solution)/shard_map/psum | solution.py:104
  538.3 18.8 %copy-start.3 = (f32[192,1536]{1,0:T(8,128)S(1)}, f32[192,1536]{1,0:T(8,128)}, u32[]{:S(2)}) copy-start(f32[192,1536]{1,0:T(8,128)} %copy-done.2) | copy-start | bytes 3538948
  566.4 2.2 copy-start
  566.4 3.6 copy-start.1
  637.4 12.9 %slice-start = ((s8[4718592]{0:T(1024)(128)(4,1)}), s8[4194304]{0:T(1024)(128)(4,1)S(1)}, s32[]{:S(2)}) async-start(s8[4718592]{0:T(1024)(128)(4,1)} %bitcast.93), calls=%async_computation.3 | async-start | bytes 8388608
  637.4 12.9 %slice-start.2 = ((s8[4718592]{0:T(1024)(128)(4,1)}), s8[4194304]{0:T(1024)(128)(4,1)S(1)}, s32[]{:S(2)}) async-start(s8[4718592]{0:T(1024)(128)(4,1)} %bitcast.95), calls=%async_computation.5 | async-start | bytes 8388608
  640.3 10.1 %slice-start.1 = ((s8[4718592]{0:T(1024)(128)(4,1)}), s8[524288]{0:T(1024)(128)(4,1)S(1)}, s32[]{:S(2)}) async-start(s8[4718592]{0:T(1024)(128)(4,1)} %bitcast.93), calls=%async_computation.4 | async-start | bytes 1048576
  640.3 10.1 %slice-start.3 = ((s8[4718592]{0:T(1024)(128)(4,1)}), s8[524288]{0:T(1024)(128)(4,1)S(1)}, s32[]{:S(2)}) async-start(s8[4718592]{0:T(1024)(128)(4,1)} %bitcast.95), calls=%async_computation.6 | async-start | bytes 1048576
  706.1 55.5 %copy-start.5 = (f32[1536]{0:T(1024)S(1)}, f32[1536]{0:T(1024)}, u32[]{:S(2)}) copy-start(f32[1536]{0:T(1024)} %copy-done.4) | copy-start | bytes 18436
Sparse Core Ops, SparseCore 0:
  580.4 57.0 all-reduce.3
where the time goes:
time: 784 us; the launch traced here: 772 us
  other arithmetic  333 us (42%)
  local copies, waits for them, and re-layouts  277 us (35%)
  matrix products  52.5 us (7%)
  waiting for transfers between devices  42.9 us (5%)
  blocking collectives  37.6 us (5%)
  between operations  15 us (2%)
  starting transfers between devices  13.8 us (2%)
    convert_element_type x1, other arithmetic, fourier_table(): jnp.cos(phases).astype(jnp.bfloat16)  105 us
    convert_element_type x1, other arithmetic, fourier_table(): (-jnp.sin(phases)).astype(jnp.bfloat16)  101 us
    another operation x2, other arithmetic, per_device(): jnp.stack([t_filter * values, weighted, degree * weighted, lowered], axis=1)  56.2 us
    rev x1, local copies, waits for them, and re-layouts, per_device(): residual.reshape(local_modes, sims_here // 2, 2, 2, degrees)[:, :, ::-1]  45.9 us
    unnamed x29, local copies, waits for them, and re-layouts  43.1 us
    psum x1, waiting for transfers between devices, per_device(): field_total = lax.psum(partial_value, 'sims')  42.9 us
    convert_element_type x1, local copies, waits for them, and re-layouts, per_device(): jnp.stack([t_filter * values, weighted, degree * weighted, lowered], axis=1)  38.3 us
    psum x1, blocking collectives, per_device(): summed = lax.psum(local_power, 'blk')  37.6 us
  transfers between devices with their start and end apart: 3, of which 1 were waited for; matrix products, arithmetic and copies ran while one was open for 31% of the time, Pallas kernels for 0%

commit v1 on v0

v1 whole, which is shorter than its diff:
```python
import functools
import math

import jax
import jax.numpy as jnp
from jax import lax
from jax.experimental import pallas as pl
from jax.experimental.pallas import tpu as pltpu
from jax.sharding import PartitionSpec as P

F32 = jnp.float32
BF16 = jnp.bfloat16
VMEM_LIMIT = 56 * 1024 * 1024


def ladder(degree, orders):
    numerator = (2.0 * degree + 1.0) * (degree * degree - orders * orders)
    denominator = jnp.maximum(2.0 * degree - 1.0, 1.0)
    return jnp.where(degree > orders, jnp.sqrt(jnp.maximum(numerator, 0.0) / denominator), 0.0)


def divisor(total, most, multiple):
    best = None
    for size in range(multiple, most + 1, multiple):
        if total % size == 0:
            best = size
    return best if best is not None else total


def trig(phase_index, period):
    k = phase_index % period
    k = jnp.where(k >= period // 2, k - period, k)
    half = k.astype(F32) * (math.pi / period)
    square = half * half

    def series(first):
        total = jnp.zeros_like(square)
        for n in reversed(range(8)):
            total = total * square + (-1.0) ** n / math.factorial(2 * n + first)
        return total

    sine = half * series(1)
    cosine = series(0)
    return 1.0 - 2.0 * sine * sine, 2.0 * sine * cosine


def legsum_kernel(alm_ref, t_ref, w_ref, leg_ref, angle_ref, first_ref, out_ref):
    block, rows, degrees = alm_ref.shape
    degree = lax.broadcasted_iota(jnp.int32, (1, degrees), 1).astype(F32)
    first = first_ref[0] + pl.program_id(0) * block
    t_filter = t_ref[...]
    w_filter = w_ref[...]
    cotangent = angle_ref[0:1, :]
    cosecant = angle_ref[1:2, :]
    parity = lax.broadcasted_iota(jnp.int32, (rows, leg_ref.shape[1]), 0) % 2
    for i in range(block):
        order = (first + i).astype(F32)
        steps = ladder(degree, order)
        values = alm_ref[i].astype(F32)
        weighted = w_filter * values
        raised = steps * weighted
        lowered = jnp.where(degree < degrees - 1, pltpu.roll(raised, degrees - 1, 1), 0.0)
        coefs = jnp.concatenate(
            [t_filter * values, weighted, degree * weighted, lowered], axis=0
        ).astype(BF16)
        sums = lax.dot_general(
            coefs, leg_ref[i], (((1,), (1,)), ((), ())), preferred_element_type=F32
        )
        wave = sums[rows : 2 * rows]
        rotated = jnp.where(
            parity == 0, -pltpu.roll(wave, rows - 1, 0), pltpu.roll(wave, 1, 0)
        ) * (cosecant * order)
        slopes = cotangent * sums[2 * rows : 3 * rows] - cosecant * sums[3 * rows :]
        out_ref[i] = jnp.concatenate([sums[:rows], rotated, slopes], axis=0)


def maps_kernel(x_ref, mask_ref, fine_ref, coarse_ref, out_ref, table, total, *, modes, scale):
    step = pl.program_id(0)
    fine = fine_ref.shape[1]
    coarse = coarse_ref.shape[1]
    rows = mask_ref.shape[0]
    fine_cos = fine_ref[0]
    fine_sin = fine_ref[1]
    for a in range(coarse):
        cos_a = coarse_ref[0, a : a + 1, :]
        sin_a = coarse_ref[1, a : a + 1, :]
        table[a * fine : (a + 1) * fine, :] = (fine_cos * cos_a - fine_sin * sin_a).astype(BF16)
        table[modes + a * fine : modes + (a + 1) * fine, :] = (
            -(fine_sin * cos_a + fine_cos * sin_a)
        ).astype(BF16)
    maps = jnp.dot(x_ref[...], table[...], preferred_element_type=F32)
    product = mask_ref[...] * maps[:rows]
    flows = jnp.concatenate(
        [product * maps[2 * rows :], product * maps[rows : 2 * rows]], axis=0
    ).astype(BF16)
    part = lax.dot_general(
        flows, table[...], (((1,), (1,)), ((), ())), preferred_element_type=F32
    )

    @pl.when(step == 0)
    def _():
        total[...] = part

    @pl.when(step > 0)
    def _():
        total[...] += part

    @pl.when(step == pl.num_programs(0) - 1)
    def _():
        out_ref[...] = (total[...] * scale).astype(BF16)


def project_kernel(x_ref, leg_ref, first_ref, field_ref, auto_ref, cross_ref):
    block = x_ref.shape[0]
    degrees = leg_ref.shape[2]
    rows = auto_ref.shape[0]
    degree = lax.broadcasted_iota(jnp.int32, (1, degrees), 1).astype(F32)
    first = first_ref[0] + pl.program_id(0) * block
    auto = jnp.zeros((rows, degrees), F32)
    cross = jnp.zeros((rows, degrees), F32)
    inverse = 1.0 / degrees

    def combine(one, two, three, steps, order):
        shifted = jnp.where(degree > 0, pltpu.roll(two, 1, 1), 0.0)
        return (degree * one - steps * shifted + order * three) * inverse

    for i in range(block):
        order = (first + i).astype(F32)
        steps = ladder(degree, order)
        leg = leg_ref[i]
        both = jnp.concatenate([leg, leg], axis=0)
        sums = jnp.dot(x_ref[i], both, preferred_element_type=F32)
        residual = combine(
            sums[:rows], sums[rows : 2 * rows], sums[2 * rows : 3 * rows], steps, order
        )
        base = 3 * rows
        field = combine(
            sums[base : base + 2], sums[base + 2 : base + 4], sums[base + 4 : base + 6], steps, order
        )
        field_ref[i] = field
        weight = jnp.where(order > 0, 2.0, 1.0)
        weighted = weight * residual
        auto = auto + weighted * residual
        cross = cross + weighted * pltpu.roll(residual, rows - 2, 0)

    @pl.when(pl.program_id(0) == 0)
    def _():
        auto_ref[...] = auto
        cross_ref[...] = cross

    @pl.when(pl.program_id(0) > 0)
    def _():
        auto_ref[...] += auto
        cross_ref[...] += cross


def params():
    return pltpu.CompilerParams(
        dimension_semantics=("arbitrary",), vmem_limit_bytes=VMEM_LIMIT
    )


def per_device(sim_alm, t_filter, wiener_filter, colatitude, legendre, pixel_mask):
    local_modes, sims_here, _, degrees = sim_alm.shape
    cycle_count = legendre.shape[2]
    pixels = pixel_mask.shape[1]
    blocks = lax.axis_size("blk")
    cycle_local = cycle_count // blocks
    modes = degrees
    first_mode = (lax.axis_index("blk") * local_modes).astype(jnp.int32).reshape(1)
    degree = jnp.arange(degrees, dtype=F32)
    rows = 2 * sims_here
    smem = pl.BlockSpec(memory_space=pltpu.SMEM)

    angles = jnp.stack([jnp.cos(colatitude) / jnp.sin(colatitude), 1.0 / jnp.sin(colatitude)])
    leg_rows = jnp.transpose(legendre, (0, 2, 1))
    block = divisor(local_modes, 8, 1)
    cycle_coefs = pl.pallas_call(
        legsum_kernel,
        grid=(local_modes // block,),
        in_specs=[
            pl.BlockSpec((block, rows, degrees), lambda i: (i, 0, 0)),
            pl.BlockSpec((1, degrees), lambda i: (0, 0)),
            pl.BlockSpec((1, degrees), lambda i: (0, 0)),
            pl.BlockSpec((block, cycle_count, degrees), lambda i: (i, 0, 0)),
            pl.BlockSpec((2, cycle_count), lambda i: (0, 0)),
            smem,
        ],
        out_specs=pl.BlockSpec((block, 3 * rows, cycle_count), lambda i: (i, 0, 0)),
        out_shape=jax.ShapeDtypeStruct((local_modes, 3 * rows, cycle_count), F32),
        compiler_params=params(),
        name="legsum",
    )(
        sim_alm.reshape(local_modes, rows, degrees),
        t_filter[None],
        wiener_filter[None],
        leg_rows,
        angles,
        first_mode,
    )

    sent = cycle_coefs.astype(BF16).reshape(local_modes, 3 * rows, blocks, cycle_local)
    sent = jnp.transpose(sent, (2, 1, 3, 0)).reshape(blocks, 3 * rows * cycle_local, local_modes)
    arrived = lax.all_to_all(sent, "blk", split_axis=0, concat_axis=0, tiled=True)
    arrived = arrived.reshape(blocks, 3 * sims_here, 2, cycle_local, local_modes)
    arrived = jnp.transpose(arrived, (1, 3, 2, 0, 4)).reshape(
        3 * sims_here * cycle_local, 2, modes
    )
    mode_weight = jnp.where(jnp.arange(modes) > 0, 2.0, 1.0).astype(BF16)
    scaled = (arrived * mode_weight).reshape(3 * sims_here * cycle_local, 2 * modes)

    map_rows = sims_here * cycle_local
    fine = divisor(modes, 64, 8)
    coarse = modes // fine
    pixel_ids = jnp.arange(pixels, dtype=jnp.int32)[None, :]
    fine_table = jnp.stack(trig(jnp.arange(fine, dtype=jnp.int32)[:, None] * pixel_ids, pixels))
    coarse_table = jnp.stack(
        trig(jnp.arange(coarse, dtype=jnp.int32)[:, None] * fine * pixel_ids, pixels)
    )
    mask_rows = jnp.tile(pixel_mask.astype(F32), (sims_here, 1))
    span = divisor(pixels, 512, 128)
    mode_coefs = pl.pallas_call(
        functools.partial(maps_kernel, modes=modes, scale=2.0 * math.pi / pixels),
        grid=(pixels // span,),
        in_specs=[
            pl.BlockSpec((3 * map_rows, 2 * modes), lambda j: (0, 0)),
            pl.BlockSpec((map_rows, span), lambda j: (0, j)),
            pl.BlockSpec((2, fine, span), lambda j: (0, 0, j)),
            pl.BlockSpec((2, coarse, span), lambda j: (0, 0, j)),
        ],
        out_specs=pl.BlockSpec((2 * map_rows, 2 * modes), lambda j: (0, 0)),
        out_shape=jax.ShapeDtypeStruct((2 * map_rows, 2 * modes), BF16),
        scratch_shapes=[
            pltpu.VMEM((2 * modes, span), BF16),
            pltpu.VMEM((2 * map_rows, 2 * modes), F32),
        ],
        compiler_params=params(),
        name="maps",
    )(scaled, mask_rows, fine_table, coarse_table)

    back = mode_coefs.reshape(2, sims_here, cycle_local, 2, blocks, local_modes)
    back = jnp.transpose(back, (4, 0, 1, 3, 2, 5)).reshape(
        blocks, 2 * rows * cycle_local, local_modes
    )
    returned = lax.all_to_all(back, "blk", split_axis=0, concat_axis=0, tiled=True)
    returned = returned.reshape(blocks, 2, sims_here, 2, cycle_local, local_modes)
    returned = jnp.transpose(returned, (5, 1, 2, 3, 0, 4)).reshape(
        local_modes, 2, sims_here, 2, cycle_count
    )
    first_flow = returned[:, 0].astype(F32)
    second_flow = returned[:, 1].astype(F32)
    tilted = (jnp.cos(colatitude) * first_flow).astype(BF16).astype(F32)
    turned = jnp.stack([second_flow[:, :, 1], -second_flow[:, :, 0]], axis=2)
    stacked = jnp.stack([tilted, first_flow, turned], axis=1)
    field_coefs = lax.psum(jnp.sum(stacked, axis=2), "sims")
    sim_total = sims_here * lax.axis_size("sims")
    centred = (stacked - field_coefs[:, :, None] / sim_total).reshape(
        local_modes, 3 * rows, cycle_count
    )
    spare = (-(3 * rows + 6)) % 8
    lines = jnp.concatenate(
        [
            centred,
            field_coefs.reshape(local_modes, 6, cycle_count),
            jnp.zeros((local_modes, spare, cycle_count), F32),
        ],
        axis=1,
    )
    upper = lax.reduce_precision(lines, 8, 7)
    lines = jnp.concatenate([upper.astype(BF16), (lines - upper).astype(BF16)], axis=2)

    height = lines.shape[1]
    field_total, auto, cross = pl.pallas_call(
        project_kernel,
        grid=(local_modes // block,),
        in_specs=[
            pl.BlockSpec((block, height, 2 * cycle_count), lambda i: (i, 0, 0)),
            pl.BlockSpec((block, cycle_count, degrees), lambda i: (i, 0, 0)),
            smem,
        ],
        out_specs=[
            pl.BlockSpec((block, 2, degrees), lambda i: (i, 0, 0)),
            pl.BlockSpec((rows, degrees), lambda i: (0, 0)),
            pl.BlockSpec((rows, degrees), lambda i: (0, 0)),
        ],
        out_shape=[
            jax.ShapeDtypeStruct((local_modes, 2, degrees), F32),
            jax.ShapeDtypeStruct((rows, degrees), F32),
            jax.ShapeDtypeStruct((rows, degrees), F32),
        ],
        compiler_params=params(),
        name="project",
    )(lines, leg_rows, first_mode)

    quarter = degrees // lax.axis_size("sims")
    field_share = lax.dynamic_slice_in_dim(
        field_total, lax.axis_index("sims") * quarter, quarter, 2
    )
    auto_power = auto.reshape(sims_here, 2, degrees).sum(axis=1)
    pair_power = cross.reshape(sims_here // 2, 2, 2, degrees)[:, 0].sum(axis=1)
    cross_power = jnp.repeat(pair_power, 2, axis=0)
    summed = lax.psum(jnp.stack([auto_power, cross_power], axis=1), "blk")
    return (field_share, summed / (2.0 * degree + 1.0))


def solution(mesh):
    placed = (P("blk", "sims", None, None), P(), P(), P(), P("blk", None, None), P("blk", None))
    return jax.shard_map(
        per_device,
        mesh=mesh,
        in_specs=placed,
        out_specs=(P("blk", None, "sims"), P("sims", None, None)),
        check_vma=False,
    )
```

time: 784 us -> 200 us (0.26); the launches traced: 772 us -> 199 us
  other arithmetic: 333 us -> 9.69 us
  local copies, waits for them, and re-layouts: 277 us -> 25 us
  Pallas kernels: 0 us -> 62 us
  matrix products: 52.5 us -> 0 us
  waiting for transfers between devices: 42.9 us -> 31.5 us
  blocking collectives: 37.6 us -> 48.7 us
    convert_element_type x6 -> x7, other arithmetic: 206 us -> 2.08 us  [the longest x1 1.82 us: per_device(): cycle_coefs.astype(BF16).reshape(local_modes, 3 * rows, blocks, cycle_local)]
    another operation x9 -> x6, other arithmetic: 68.3 us -> 3.08 us  [the longest x1 1.48 us: per_device(): jnp.stack(trig(jnp.arange(fine, dtype=jnp.int32)[:, None] * pixel_ids, pi...]
    pallas_call x0 -> x3, Pallas kernels: none -> 62 us  [the longest x1 23 us: per_device(): pl.pallas_call(project_kernel, grid=(local_modes // block,), in_specs=[pl...]
    dot_general x6 -> x0, matrix products: 52.5 us -> none  [the longest x1 17.5 us: per_device(): jnp.einsum('kscbnr,nlbr->knscl', stacked, legendre_grid, preferred_elemen...]
    another operation x9 -> x3, local copies, waits for them, and re-layouts: 52.8 us -> 0.8 us  [the longest x2 0.78 us: per_device(): mask_rows = jnp.tile(pixel_mask.astype(F32), (sims_here, 1))]
    rev x1 -> x0, local copies, waits for them, and re-layouts: 45.9 us -> none  [per_device(): residual.reshape(local_modes, sims_here // 2, 2, 2, degrees)[:, :, ::-1]]
    unnamed x29 -> x8, local copies, waits for them, and re-layouts: 43.1 us -> 1.38 us
    convert_element_type x2 -> x1, local copies, waits for them, and re-layouts: 41 us -> 0.78 us  [per_device(): cycle_coefs.astype(BF16).reshape(local_modes, 3 * rows, blocks, cycle_local)]
  transfers between devices with their start and end apart: 3 -> 2, of which waited for: 1 -> 2; matrix products, arithmetic and copies ran while one was open for 31% -> 3% of each run, Pallas kernels for 0% -> 0%
where the time goes in v1:
time: 200 us; the launch traced here: 199 us
  Pallas kernels  62 us (31%)
  blocking collectives  48.7 us (24%)
  waiting for transfers between devices  31.5 us (16%)
  local copies, waits for them, and re-layouts  25 us (12%)
  between operations  14.3 us (7%)
  other arithmetic  9.69 us (5%)
  starting transfers between devices  7.35 us (4%)
    psum x1, blocking collectives, per_device(): summed = lax.psum(jnp.stack([auto_power, cross_power], axis=1), 'blk')  37.6 us
    psum x1, waiting for transfers between devices, per_device(): field_coefs = lax.psum(jnp.sum(stacked, axis=2), 'sims')  29.5 us
    pallas_call x1, Pallas kernels, per_device(): pl.pallas_call(project_kernel, grid=(local_modes // block,), in_specs=[pl...  23 us
    pallas_call x1, Pallas kernels, per_device(): pl.pallas_call(legsum_kernel, grid=(local_modes // block,), in_specs=[pl....  21.5 us
    pallas_call x1, Pallas kernels, per_device(): pl.pallas_call(functools.partial(maps_kernel, modes=modes, scale=2.0 * ma...  17.5 us
    all_to_all x1, blocking collectives, per_device(): lax.all_to_all(back, 'blk', split_axis=0, concat_axis=0, tiled=True)  11.1 us
    reshape x1, local copies, waits for them, and re-layouts, per_device(): sim_alm.reshape(local_modes, rows, degrees)  10.7 us
    all_to_all x1, starting transfers between devices, per_device(): lax.all_to_all(sent, 'blk', split_axis=0, concat_axis=0, tiled=True)  7.31 us
  transfers between devices with their start and end apart: 2, of which 2 were waited for; matrix products, arithmetic and copies ran while one was open for 3% of the time, Pallas kernels for 0%

profile of v1, /device:TPU:0, one launch (start us, length us, event | category | flops | bytes accessed | tf_op | source)
XLA Modules:
  0.0 198.5 jit_solution(6733780951408050603)
XLA Ops:
  7.2 0.7 fusion.33
  7.9 10.7 %reshape.468.alm_ref = bf16[192,8,1536]{2,1,0:T(8,128)(2,1)} reshape(bf16[192,4,2,1536]{3,2,1,0:T(2,128)(2,1)} %param.6) | data formatting | bytes 9437184 | tf_op jit(solution)/shard_map/reshape | solution.py:194
  18.6 0.6 broadcast_in_dim.27.t_ref
  19.2 0.6 broadcast_in_dim.28.w_ref
  19.8 0.6 pad_maximum_fusion.5.angle_ref
  20.4 21.5 %legsum.1 = f32[192,24,16]{2,1,0:T(8,128)} custom-call(bf16[192,8,1536]{2,1,0:T(8,128)(2,1)} %reshape.468.alm_ref, f32[1,1536]{1,0:T(1,128)} %broadcast_in_dim.27.t_ref, f32[1,1536]{1,0:T(1,128)} %broadcast_in_dim.28.w_ref, bf16[192,16,1536]{2,1,0:T(8,128)(2,1)} %bitcast.32, f32[2,16]{1,0:T(2,128)} %pad_maximum_fusion.5.angle_ref, s32[1]{0:T(128)} %bitcast.3.first_ref), custom_call_target="tpu_custom_call" | custom-call | tf_op jit(solution)/shard_map/legsum/pallas_call | solution.py:178
  41.8 1.8 convert_element_type.70
  43.7 0.8 copy.44
  44.5 0.7 copy.46
  45.2 7.3 %all-to-all-start = ((bf16[8,48,192]{2,1,0:T(8,128)(2,1)}), bf16[8,48,192]{2,1,0:T(8,128)(2,1)S(1)}, u32[]{:S(2)}, u32[]{:S(2)}) async-start(bf16[8,48,192]{2,1,0:T(8,128)(2,1)} %copy.46), calls=%async_computation | async-start | bytes 393216 | tf_op jit(solution)/shard_map/all_to_all | solution.py:204
  52.6 1.8 multiply_multiply_fusion
  54.5 0.8 fusion.14
  55.3 0.7 tile.10.mask_ref
  56.1 1.5 pad_maximum_fusion.fine_ref
  57.6 1.0 pad_maximum_fusion.1.coarse_ref
  58.5 2.0 all-to-all-done
  60.6 0.2 reshape.473
  60.8 0.7 broadcast_multiply_fusion.x_ref
  61.5 17.5 %maps.1 = bf16[16,3072]{1,0:T(8,128)(2,1)} custom-call(bf16[24,3072]{1,0:T(8,128)(2,1)} %broadcast_multiply_fusion.x_ref, f32[8,4096]{1,0:T(8,128)} %tile.10.mask_ref, f32[2,64,4096]{2,1,0:T(8,128)} %pad_maximum_fusion.fine_ref, f32[2,24,4096]{2,1,0:T(8,128)} %pad_maximum_fusion.1.coarse_ref), custom_call_target="tpu_custom_call" | custom-call | tf_op jit(solution)/shard_map/maps/pallas_call | solution.py:222
  79.0 1.1 reshape.474
  80.2 11.1 %all_to_all.10 = bf16[8,32,192]{2,1,0:T(8,128)(2,1)S(1)} all-to-all(bf16[8,32,192]{2,1,0:T(8,128)(2,1)S(1)} %copy.50), channel_id=1, replica_groups=mesh['sims'=4,'blk'=8] {'blk'}, dimensions={0} | all-to-all | bytes 196608 | tf_op jit(solution)/shard_map/all_to_all | solution.py:245
  91.8 0.7 copy.60
  92.6 29.5 %all-reduce.2.cloned.1.call-done = f32[192,3,2,16]{0,2,3,1:T(2,128)} async-done(((f32[192,3,2,16]{0,2,3,1:T(2,128)}), f32[192,3,2,16]{0,2,3,1:T(2,128)}) %all-reduce.2.cloned.1.call-update) | async-done | bytes 73744 | tf_op jit(solution)/shard_map/psum | solution.py:255
  122.1 0.9 broadcast_multiply_fusion.1
  123.1 0.9 copy.57
  124.3 2.2 %copy.58.x_ref = bf16[192,32,32]{2,1,0:T(8,128)(2,1)} copy(bf16[192,32,32]{0,2,1:T(8,128)(2,1)S(1)} %pad_maximum_fusion.2) | data formatting | bytes 786432 | tf_op jit(solution)/shard_map/concatenate | solution.py:270
  126.5 23.0 %project.1 = (f32[192,2,1536]{2,1,0:T(2,128)}, f32[8,1536]{1,0:T(8,128)}, f32[8,1536]{1,0:T(8,128)}) custom-call(bf16[192,32,32]{2,1,0:T(8,128)(2,1)} %copy.58.x_ref, bf16[192,16,1536]{2,1,0:T(8,128)(2,1)} %bitcast.33, s32[1]{0:T(128)} %bitcast.3.first_ref), custom_call_target="tpu_custom_call" | custom-call | tf_op jit(solution)/shard_map/project/pallas_call | solution.py:273
  149.5 0.8 reshape.480
  150.4 0.8 reshape.479
  151.4 37.6 %psum.15 = f32[4,2,1536]{2,0,1:T(4,128)S(1)} all-reduce(f32[4,2,1536]{2,0,1:T(4,128)S(1)} %pad_maximum_fusion.4), channel_id=1, replica_groups=mesh['sims'=4,'blk'=8] {'blk'}, use_global_device_ids=true, to_apply=%region_4.5 | all-reduce | flops 12288 | bytes 98304 | tf_op jit(solution)/shard_map/psum | solution.py:302
  189.0 0.6 copy.59
  189.6 2.1 %constant_dynamic-slice_fusion = f32[192,2,384]{2,1,0:T(2,128)} fusion(f32[192,2,1536]{2,1,0:T(2,128)} %get-tuple-element.5, s32[]{:T(128)S(6)} %select_n.89), kind=kLoop, calls=%fused_computation.81 | loop fusion | bytes 1179652 | tf_op jit(solution)/shard_map/dynamic_slice | solution.py:296
  (42 shorter events, 1.3 us)
Async XLA Ops:
  7.9 10.7 %copy-start.1 = (f32[1536]{0:T(1024)S(1)}, f32[1536]{0:T(1024)}, u32[]{:S(2)}) copy-start(f32[1536]{0:T(1024)} %param.7) | copy-start | bytes 18436
  7.9 11.3 %copy-start.2 = (f32[1536]{0:T(1024)S(1)}, f32[1536]{0:T(1024)}, u32[]{:S(2)}) copy-start(f32[1536]{0:T(1024)} %param.8) | copy-start | bytes 18436
  44.4 10.8 %copy-start = (s32[2,4096]{1,0:T(2,128)S(1)}, s32[2,4096]{1,0:T(2,128)}, u32[]{:S(2)}) copy-start(s32[2,4096]{1,0:T(2,128)} %param.11) | copy-start | bytes 98308
  45.2 15.3 %all-to-all-start = ((bf16[8,48,192]{2,1,0:T(8,128)(2,1)}), bf16[8,48,192]{2,1,0:T(8,128)(2,1)S(1)}, u32[]{:S(2)}, u32[]{:S(2)}) async-start(bf16[8,48,192]{2,1,0:T(8,128)(2,1)} %copy.46), calls=%async_computation | async-start | bytes 393216 | tf_op jit(solution)/shard_map/all_to_all | solution.py:204
  52.6 69.6 %all-reduce.2.cloned.1.call-start = ((), (), s32[]{:S(2)}) async-start(), calls=%async_computation.2 | async-start | bytes 196608 | tf_op jit(solution)/shard_map/psum | solution.py:255
Sparse Core Ops, SparseCore 0:
  92.7 29.4 all-reduce.1
